TPU v7x, 32 devices: a whole 2x2x4 slice. The times are simulated.
32 devices in a mesh: blk: 8 (over y, x, core), uly: 4 (over z).
Axes of the slice: x: 2, y: 2, z: 4, core: 2. Of those that a mesh axis runs over, the one named last changes fastest.
Arguments:
- qkv: bfloat16 [2048, 3, 3072], P(('blk', 'uly')), may hold values from -9 to 9
Outputs:
- attended: float32 [2048, 3072], P('blk', 'uly')
- log_total: float32 [24, 2048], P('uly', 'blk')
All inputs are finite; a program needn't handle non-finite values.
Results may differ from a plain program's by a relative error of at most 0.0027.
Values may be sent and summed in bfloat16 or wider, within the bound.
No kernel may reach another device: no remote copies, remote signals or barrier semaphores. Data moves between devices by JAX's collectives and lax.ppermute only.
A program may use at most 64 MiB of HBM per device.

v0:
```python
import math
import jax
import jax.numpy as jnp
from jax import lax
from jax.sharding import PartitionSpec as P

HEAD_DIM = 128


def from_behind(value, axis, steps):
    count = lax.axis_size(axis)
    pairs = [(source, (source + steps) % count) for source in range(count)]
    return lax.ppermute(value, axis, pairs)


def block_scores(query_rows, key_rows, temper):
    return (
        jnp.einsum("rhd,khd->hrk", query_rows, key_rows, preferred_element_type=jnp.float32)
        * temper
    )


def attend_first(query_rows, key_rows, value_rows, temper):
    scores = block_scores(query_rows, key_rows, temper)
    top = jnp.max(scores, axis=2)
    weights = jnp.exp(scores - top[:, :, None])
    total = jnp.sum(weights, axis=2)
    accum = jnp.einsum(
        "hrk,khd->hrd", weights.astype(jnp.bfloat16), value_rows, preferred_element_type=jnp.float32
    )
    return (top, total, accum)


def attend_next(running, query_rows, key_rows, value_rows, temper):
    top, total, accum = running
    scores = block_scores(query_rows, key_rows, temper)
    newtop = jnp.maximum(top, jnp.max(scores, axis=2))
    factor = jnp.exp(top - newtop)
    weights = jnp.exp(scores - newtop[:, :, None])
    total = total * factor + jnp.sum(weights, axis=2)
    accum = accum * factor[:, :, None] + jnp.einsum(
        "hrk,khd->hrd", weights.astype(jnp.bfloat16), value_rows, preferred_element_type=jnp.float32
    )
    return (newtop, total, accum)


def shards(qkv):
    width = qkv.shape[2] // lax.axis_size("uly")
    heads_local = width // HEAD_DIM
    temper = 1.0 / math.sqrt(HEAD_DIM)
    grouped = lax.all_to_all(qkv, "uly", split_axis=2, concat_axis=0, tiled=True)
    prev_pairs = from_behind(grouped[:, 1:], "blk", 1)
    block_len = grouped.shape[0]
    row_count = math.gcd(block_len, 512)
    queries = grouped[:, 0].reshape(block_len // row_count, row_count, heads_local, HEAD_DIM)
    own_keys = grouped[:, 1].reshape(block_len, heads_local, HEAD_DIM)
    own_values = grouped[:, 2].reshape(block_len, heads_local, HEAD_DIM)
    prev_keys = prev_pairs[:, 0].reshape(block_len, heads_local, HEAD_DIM)
    prev_values = prev_pairs[:, 1].reshape(block_len, heads_local, HEAD_DIM)

    def per_rows(query_rows):
        running = attend_first(query_rows, own_keys, own_values, temper)
        top, total, accum = attend_next(running, query_rows, prev_keys, prev_values, temper)
        normed = accum / total[:, :, None]
        return (jnp.transpose(normed, (1, 0, 2)).reshape(row_count, width), top + jnp.log(total))

    attended_rows, log_rows = lax.map(per_rows, queries)
    attended = attended_rows.reshape(block_len, width)
    log_total = jnp.transpose(log_rows, (1, 0, 2)).reshape(heads_local, block_len)
    return (attended, log_total)


def solution(mesh):
    placed = (P(("blk", "uly"), None, None),)
    return jax.shard_map(
        shards,
        mesh=mesh,
        in_specs=placed,
        out_specs=(P("blk", "uly"), P("uly", "blk")),
        check_vma=False,
    )
```

profile of v0, /device:TPU:0, one launch (start us, length us, event | category | flops | bytes accessed | tf_op | source)
XLA Modules:
  0.0 74.6 jit_solution(17815620228269308837)
XLA Ops:
  0.6 4.6 %copy.32 = bf16[64,3,3072]{0,1,2:T(4,128)(2,1)S(1)} copy(bf16[64,3,3072]{2,0,1:T(8,128)(2,1)} %param.1) | data formatting | bytes 2359296 | tf_op args[0]
  5.2 3.1 %reshape.40 = bf16[4,2,73728]{2,1,0:T(2,128)(2,1)} reshape(bf16[3072,3,64]{2,1,0:T(4,128)(2,1)S(1)} %bitcast.42) | data formatting | bytes 2359296
  8.3 35.0 %all_to_all.18 = bf16[4,2,73728]{2,1,0:T(2,128)(2,1)} all-to-all(bf16[4,2,73728]{2,1,0:T(2,128)(2,1)} %reshape.40), channel_id=1, replica_groups=mesh['blk'=8,'uly'=4] {'uly'}, dimensions={0} | all-to-all | bytes 2359296 | tf_op jit(solution)/shard_map/all_to_all | solution.py:51
  43.2 3.5 %reshape.41 = bf16[3072,3,64]{2,1,0:T(4,128)(2,1)S(1)} reshape(bf16[4,2,73728]{2,1,0:T(2,128)(2,1)} %all_to_all.18) | data formatting | bytes 2359296
  46.7 3.2 %copy.34 = bf16[4,64,3,768]{3,1,0,2:T(8,128)(2,1)} copy(bf16[4,64,3,768]{1,2,3,0:T(4,128)(2,1)S(1)} %bitcast.41) | data formatting | bytes 2359296 | tf_op jit(solution)/shard_map/all_to_all | solution.py:51
  49.9 0.0 copy-start
  49.9 2.2 %slice.27 = bf16[256,2,768]{2,0,1:T(8,128)(2,1)} slice(bf16[256,3,768]{2,0,1:T(8,128)(2,1)} %bitcast.43), slice={[0:256], [1:3], [0:768]} | slice | bytes 1572864 | tf_op jit(solution)/shard_map/slice | solution.py:52
  52.1 0.0 collective-permute-start
  52.1 0.0 copy-done
  52.1 0.1 fusion.13
  52.2 0.2 copy.36
  52.3 0.9 %copy.39 = bf16[256,1,768]{0,2,1:T(8,128)(2,1)} copy(bf16[256,1,768]{2,0,1:T(8,128)(2,1)S(1)} %get-tuple-element.37) | data formatting | bytes 786432 | tf_op jit(solution)/shard_map/slice | solution.py:57
  53.2 0.2 copy.35
  53.4 0.4 fusion.15
  53.8 10.9 %collective-permute-done = bf16[256,2,768]{2,0,1:T(8,128)(2,1)} collective-permute-done((bf16[256,2,768]{2,0,1:T(8,128)(2,1)}, bf16[256,2,768]{2,0,1:T(8,128)(2,1)}, u32[]{:S(2)}, u32[]{:S(2)}) %collective-permute-start) | collective-permute-done | bytes 786464 | tf_op jit(solution)/shard_map/ppermute | solution.py:13
  64.7 1.9 %fusion.14 = (bf16[256,1,768]{2,0,1:T(8,128)(2,1)}, bf16[256,1,768]{2,0,1:T(8,128)(2,1)S(1)}) fusion(bf16[256,2,768]{2,0,1:T(8,128)(2,1)} %collective-permute-done), kind=kLoop, calls=%fused_computation.21 | loop fusion | bytes 1572864 | tf_op jit(solution)/shard_map/slice | solution.py:59
  66.6 0.9 %copy.41 = bf16[256,1,768]{0,2,1:T(8,128)(2,1)} copy(bf16[256,1,768]{2,0,1:T(8,128)(2,1)S(1)} %get-tuple-element.40) | data formatting | bytes 786432 | tf_op jit(solution)/shard_map/slice | solution.py:58
  67.5 1.4 %fusion.16 = (f32[6,256]{1,0:T(8,128)S(1)}, f32[6,256,256]{1,2,0:T(8,128)S(1)}) fusion(bf16[256,6,128]{0,2,1:T(8,128)(2,1)S(1)} %bitcast.46, bf16[256,6,128]{0,2,1:T(8,128)(2,1)} %bitcast.48), kind=kOutput, calls=%fused_computation.23 | convolution fusion | flops 101448192 | bytes 2365440 | tf_op jit(solution)/shard_map/while/body/eval_jaxpr/rhd,khd->hrk/dot_general | solution.py:18
  69.0 0.0 copy-start.1
  69.0 0.4 fusion
  69.4 0.6 log_add_fusion
  70.0 0.6 bitcast_add_fusion
  70.7 0.0 copy-done.1
  70.7 0.9 %copy.44 = bf16[256,1,768]{0,2,1:T(8,128)(2,1)} copy(bf16[256,1,768]{2,0,1:T(8,128)(2,1)S(1)} %copy-done.1) | data formatting | bytes 786432 | tf_op jit(solution)/shard_map/slice | solution.py:59
  71.6 0.0 copy-start.2
  71.6 0.0 copy-start.3
  71.6 1.5 %fusion.4 = f32[256,6,128]{0,2,1:T(8,128)S(1)} fusion(bf16[256,6,128]{0,2,1:T(8,128)(2,1)} %bitcast.49, f32[6,256,256]{1,2,0:T(8,128)S(1)} %get-tuple-element.42, f32[6,256]{1,0:T(8,128)S(1)} %get-tuple-element.41, f32[256,6]{0,1:T(8,128)} %get-tuple-element.35), kind=kOutput, calls=%fused_computation.10 | convolution fusion | flops 101646336 | bytes 2764800 | tf_op jit(solution)/shard_map/while/body/eval_jaxpr/hrk,khd->hrd/dot_general | solution.py:28
  73.0 0.0 copy-done.2
  73.0 0.0 copy-done.3
  73.1 0.4 fusion.6
  73.5 1.1 %copy.46 = f32[256,768]{1,0:T(8,128)} copy(f32[256,768]{0,1:T(8,128)S(1)} %bitcast.50) | data formatting | bytes 1572864
  (1 shorter events, 0.0 us)
Async XLA Ops:
  49.9 2.2 %copy-start = (bf16[4,64,3,768]{3,1,0,2:T(8,128)(2,1)S(1)}, bf16[4,64,3,768]{3,1,0,2:T(8,128)(2,1)}, u32[]{:S(2)}) copy-start(bf16[4,64,3,768]{3,1,0,2:T(8,128)(2,1)} %copy.34) | copy-start | bytes 3538948
  52.1 12.6 %collective-permute-start = (bf16[256,2,768]{2,0,1:T(8,128)(2,1)}, bf16[256,2,768]{2,0,1:T(8,128)(2,1)}, u32[]{:S(2)}, u32[]{:S(2)}) collective-permute-start(bf16[256,2,768]{2,0,1:T(8,128)(2,1)} %slice.27), channel_id=1, source_target_pairs={{0,4},{4,8},{8,12},{12,16},{16,20},{20,24},{24,28},{28,0},{1,5},{5... | collective-permute-start | bytes 2359304 | tf_op jit(solution)/shard_map/ppermute | solution.py:13
  69.0 1.7 %copy-start.1 = (bf16[256,1,768]{2,0,1:T(8,128)(2,1)S(1)}, bf16[256,1,768]{2,0,1:T(8,128)(2,1)}, u32[]{:S(2)}) copy-start(bf16[256,1,768]{2,0,1:T(8,128)(2,1)} %get-tuple-element.39) | copy-start | bytes 1179652
  71.6 1.5 %copy-start.2 = (bf16[256,1,768]{0,2,1:T(8,128)(2,1)S(1)}, bf16[256,1,768]{0,2,1:T(8,128)(2,1)}, u32[]{:S(2)}) copy-start(bf16[256,1,768]{0,2,1:T(8,128)(2,1)} %copy.44) | copy-start | bytes 1179652
  71.6 1.5 %copy-start.3 = (f32[256,6]{0,1:T(8,128)S(1)}, f32[256,6]{0,1:T(8,128)}, u32[]{:S(2)}) copy-start(f32[256,6]{0,1:T(8,128)} %get-tuple-element.34) | copy-start | bytes 18436
where the time goes:
time: 75 us; the launch traced here: 74.6 us
  blocking collectives  35 us (47%)
  local copies, waits for them, and re-layouts  22.7 us (30%)
  waiting for transfers between devices  10.9 us (15%)
  matrix products  3.71 us (5%)
  other arithmetic  1.68 us (2%)
    all_to_all x1, blocking collectives, shards(): lax.all_to_all(qkv, 'uly', split_axis=2, concat_axis=0, tiled=True)  35 us
    unnamed x12, local copies, waits for them, and re-layouts  12.3 us
    ppermute x1, waiting for transfers between devices, from_behind(): return lax.ppermute(value, axis, pairs)  10.9 us
    all_to_all x1, local copies, waits for them, and re-layouts, shards(): lax.all_to_all(qkv, 'uly', split_axis=2, concat_axis=0, tiled=True)  3.21 us
    slice x2, local copies, waits for them, and re-layouts, shards(): prev_values = prev_pairs[:, 1].reshape(block_len, heads_local, HEAD_DIM)  2.83 us
    slice x1, local copies, waits for them, and re-layouts, shards(): prev_pairs = from_behind(grouped[:, 1:], 'blk', 1)  2.16 us
    dot_general x2, matrix products, block_scores(): jnp.einsum('rhd,khd->hrk', query_rows, key_rows, preferred_element_type=j...  1.84 us
  transfers between devices with their start and end apart: 1, of which 1 were waited for; matrix products, arithmetic and copies ran while one was open for 2% of the time, Pallas kernels for 0%

commit v1 on v0

--- a/solution.py
+++ b/solution.py
@@ -48,7 +48,9 @@
     width = qkv.shape[2] // lax.axis_size("uly")
     heads_local = width // HEAD_DIM
     temper = 1.0 / math.sqrt(HEAD_DIM)
-    grouped = lax.all_to_all(qkv, "uly", split_axis=2, concat_axis=0, tiled=True)
+    grouped = jnp.concatenate(
+        lax.all_to_all(jnp.stack(jnp.split(qkv, lax.axis_size("uly"), axis=2)), "uly", 0, 0), axis=0
+    )
     prev_pairs = from_behind(grouped[:, 1:], "blk", 1)
     block_len = grouped.shape[0]
     row_count = math.gcd(block_len, 512)

time: 75 us -> 59.4 us (0.79)
  local copies, waits for them, and re-layouts: 22.7 us -> 7.45 us
    unnamed x12 -> x7, local copies, waits for them, and re-layouts: 12.3 us -> 1.16 us
    all_to_all x1, local copies, waits for them, and re-layouts: 3.21 us -> 0.08 us  [shards(): lax.all_to_all(jnp.stack(jnp.split(qkv, lax.axis_size('uly'), axis=2)), '...]
    another operation x0 -> x1, local copies, waits for them, and re-layouts: none -> 1.32 us  [shards(): jnp.stack(jnp.split(qkv, lax.axis_size('uly'), axis=2))]
    slice x1, local copies, waits for them, and re-layouts: 2.16 us -> 0.93 us  [shards(): prev_pairs = from_behind(grouped[:, 1:], 'blk', 1)]
    slice x2, local copies, waits for them, and re-layouts: 2.83 us -> 1.71 us  [shards(): prev_values = prev_pairs[:, 1].reshape(block_len, heads_local, HEAD_DIM)]
  transfers between devices with their start and end apart: 1 -> 1, of which waited for: 1 -> 1; matrix products, arithmetic and copies ran while one was open for 2% -> 3% of each run, Pallas kernels for 0% -> 0%
where the time goes in v1:
time: 59.4 us; the launch traced here: 59.2 us
  blocking collectives  34.7 us (58%)
  waiting for transfers between devices  10.7 us (18%)
  local copies, waits for them, and re-layouts  7.45 us (13%)
  matrix products  3.72 us (6%)
  other arithmetic  1.86 us (3%)
  between operations  0.74 us (1%)
    all_to_all x1, blocking collectives, shards(): lax.all_to_all(jnp.stack(jnp.split(qkv, lax.axis_size('uly'), axis=2)), '...  34.7 us
    ppermute x1, waiting for transfers between devices, from_behind(): return lax.ppermute(value, axis, pairs)  10.7 us
    dot_general x2, matrix products, block_scores(): jnp.einsum('rhd,khd->hrk', query_rows, key_rows, preferred_element_type=j...  1.85 us
    slice x2, local copies, waits for them, and re-layouts, shards(): prev_values = prev_pairs[:, 1].reshape(block_len, heads_local, HEAD_DIM)  1.71 us
    dot_general x1, matrix products, attend_first(): jnp.einsum('hrk,khd->hrd', weights.astype(jnp.bfloat16), value_rows, pref...  1.45 us
    another operation x1, local copies, waits for them, and re-layouts, shards(): jnp.stack(jnp.split(qkv, lax.axis_size('uly'), axis=2))  1.32 us
  transfers between devices with their start and end apart: 1, of which 1 were waited for; matrix products, arithmetic and copies ran while one was open for 3% of the time, Pallas kernels for 0%

profile of v1, /device:TPU:0, one launch (start us, length us, event | category | flops | bytes accessed | tf_op | source)
XLA Modules:
  0.0 59.2 jit_solution(17559278944117453613)
XLA Ops:
  0.6 1.3 %slice_bitcast_fusion.3 = (bf16[1,64,3,768]{3,1,2,0:T(8,128)(2,1)S(1)}, bf16[1,64,3,768]{3,1,2,0:T(8,128)(2,1)S(1)}, bf16[1,64,3,768]{3,1,2,0:T(8,128)(2,1)S(1)}, bf16[1,64,3,768]{3,1,2,0:T(8,128)(2,1)S(1)}) fusion(bf16[64,3,3072]{2,0,1:T(8,128)(2,1)} %param.1), kind=kLoop, calls=%fused_computation.19 | loop fusion | bytes 2359296 | tf_op jit(solution)/shard_map/stack | solution.py:52
  2.0 0.2 pad_maximum_fusion
  2.1 34.7 %all_to_all.5 = bf16[4,64,3,768]{3,1,2,0:T(8,128)(2,1)S(1)} all-to-all(bf16[4,64,3,768]{3,1,2,0:T(8,128)(2,1)S(1)} %pad_maximum_fusion), channel_id=1, replica_groups=mesh['blk'=8,'uly'=4] {'uly'}, dimensions={0} | all-to-all | bytes 2359296 | tf_op jit(solution)/shard_map/all_to_all | solution.py:52
  36.8 0.1 copy.18
  36.9 0.9 %slice.27 = bf16[256,2,768]{2,0,1:T(8,128)(2,1)} slice(bf16[256,3,768]{2,0,1:T(8,128)(2,1)S(1)} %bitcast.43), slice={[0:256], [1:3], [0:768]} | slice | bytes 1572864 | tf_op jit(solution)/shard_map/slice | solution.py:54
  37.8 0.0 collective-permute-start
  37.8 0.1 fusion.13
  37.9 0.2 copy.20
  38.0 0.9 %copy.23 = bf16[256,1,768]{0,2,1:T(8,128)(2,1)} copy(bf16[256,1,768]{2,0,1:T(8,128)(2,1)S(1)} %get-tuple-element.35) | data formatting | bytes 786432 | tf_op jit(solution)/shard_map/slice | solution.py:59
  39.0 0.2 copy.19
  39.1 0.4 fusion.15
  39.6 10.7 %collective-permute-done = bf16[256,2,768]{2,0,1:T(8,128)(2,1)S(1)} collective-permute-done((bf16[256,2,768]{2,0,1:T(8,128)(2,1)}, bf16[256,2,768]{2,0,1:T(8,128)(2,1)S(1)}, u32[]{:S(2)}, u32[]{:S(2)}) %collective-permute-start) | collective-permute-done | bytes 786464 | tf_op jit(solution)/shard_map/ppermute | solution.py:13
  50.3 0.8 %fusion.14 = (bf16[256,1,768]{2,0,1:T(8,128)(2,1)}, bf16[256,1,768]{2,0,1:T(8,128)(2,1)S(1)}) fusion(bf16[256,2,768]{2,0,1:T(8,128)(2,1)S(1)} %collective-permute-done), kind=kLoop, calls=%fused_computation.26 | loop fusion | bytes 1572864 | tf_op jit(solution)/shard_map/slice | solution.py:61
  51.1 0.9 %copy.25 = bf16[256,1,768]{0,2,1:T(8,128)(2,1)} copy(bf16[256,1,768]{2,0,1:T(8,128)(2,1)S(1)} %get-tuple-element.42) | data formatting | bytes 786432 | tf_op jit(solution)/shard_map/slice | solution.py:60
  52.0 1.4 %fusion.16 = (f32[6,256]{1,0:T(8,128)S(1)}, f32[6,256,256]{1,2,0:T(8,128)S(1)}) fusion(bf16[256,6,128]{0,2,1:T(8,128)(2,1)S(1)} %bitcast.46, bf16[256,6,128]{0,2,1:T(8,128)(2,1)} %bitcast.48), kind=kOutput, calls=%fused_computation.28 | convolution fusion | flops 101448192 | bytes 2365440 | tf_op jit(solution)/shard_map/while/body/eval_jaxpr/rhd,khd->hrk/dot_general | solution.py:18
  53.5 0.0 copy-start
  53.5 0.5 fusion
  53.9 0.6 %log_add_fusion = f32[6,256]{1,0:T(8,128)} fusion(f32[6,256]{1,0:T(8,128)S(1)} %max.20, f32[6,256]{1,0:T(8,128)S(1)} %get-tuple-element.48, f32[6,256]{1,0:T(8,128)S(1)} %get-tuple-element.47, f32[6,256]{1,0:T(8,128)S(1)} %get-tuple-element.43), kind=kLoop, calls=%fused_computation.24 | loop fusion | flops 6144 | bytes 30720 | tf_op jit(solution)/shard_map/while/body/eval_jaxpr/add | solution.py:67
  54.6 0.6 %bitcast_add_fusion = (f32[256,6]{0,1:T(8,128)}, f32[256,6]{0,1:T(8,128)}) fusion(f32[6,256]{1,0:T(8,128)S(1)} %get-tuple-element.48, f32[6,256]{1,0:T(8,128)S(1)} %get-tuple-element.47, f32[6,256]{1,0:T(8,128)S(1)} %get-tuple-element.45, f32[6,256]{1,0:T(8,128)S(1)} %get-tuple-element.43), kind=kLoop, calls=%fused_computation.22 | loop fusion | flops 6144 | bytes 36864 | tf_op jit(solution)/shard_map/while/body/eval_jaxpr/add | solution.py:40
  55.2 0.0 copy-done
  55.2 0.9 %copy.28 = bf16[256,1,768]{0,2,1:T(8,128)(2,1)} copy(bf16[256,1,768]{2,0,1:T(8,128)(2,1)S(1)} %copy-done) | data formatting | bytes 786432 | tf_op jit(solution)/shard_map/slice | solution.py:61
  56.1 0.0 copy-start.1
  56.1 0.0 copy-start.2
  56.1 1.5 %fusion.4 = f32[256,6,128]{0,2,1:T(8,128)S(1)} fusion(bf16[256,6,128]{0,2,1:T(8,128)(2,1)} %bitcast.49, f32[6,256,256]{1,2,0:T(8,128)S(1)} %get-tuple-element.44, f32[6,256]{1,0:T(8,128)S(1)} %get-tuple-element.43, f32[256,6]{0,1:T(8,128)} %get-tuple-element.33), kind=kOutput, calls=%fused_computation.10 | convolution fusion | flops 101646336 | bytes 2764800 | tf_op jit(solution)/shard_map/while/body/eval_jaxpr/hrk,khd->hrd/dot_general | solution.py:28
  57.6 0.0 copy-done.1
  57.6 0.0 copy-done.2
  57.6 0.4 fusion.6
  58.0 1.1 %copy.30 = f32[256,768]{1,0:T(8,128)} copy(f32[256,768]{0,1:T(8,128)S(1)} %bitcast.50) | data formatting | bytes 1572864
  (1 shorter events, 0.0 us)
Async XLA Ops:
  37.8 12.5 %collective-permute-start = (bf16[256,2,768]{2,0,1:T(8,128)(2,1)}, bf16[256,2,768]{2,0,1:T(8,128)(2,1)S(1)}, u32[]{:S(2)}, u32[]{:S(2)}) collective-permute-start(bf16[256,2,768]{2,0,1:T(8,128)(2,1)} %slice.27), channel_id=1, source_target_pairs={{0,4},{4,8},{8,12},{12,16},{16,20},{20,24},{24,28},{28,0},{1,5},{5... | collective-permute-start | bytes 2359304 | tf_op jit(solution)/shard_map/ppermute | solution.py:13
  53.5 1.7 %copy-start = (bf16[256,1,768]{2,0,1:T(8,128)(2,1)S(1)}, bf16[256,1,768]{2,0,1:T(8,128)(2,1)}, u32[]{:S(2)}) copy-start(bf16[256,1,768]{2,0,1:T(8,128)(2,1)} %get-tuple-element.41) | copy-start | bytes 1179652
  56.1 1.5 %copy-start.1 = (bf16[256,1,768]{0,2,1:T(8,128)(2,1)S(1)}, bf16[256,1,768]{0,2,1:T(8,128)(2,1)}, u32[]{:S(2)}) copy-start(bf16[256,1,768]{0,2,1:T(8,128)(2,1)} %copy.28) | copy-start | bytes 1179652
  56.1 1.5 %copy-start.2 = (f32[256,6]{0,1:T(8,128)S(1)}, f32[256,6]{0,1:T(8,128)}, u32[]{:S(2)}) copy-start(f32[256,6]{0,1:T(8,128)} %get-tuple-element.32) | copy-start | bytes 18436
